TPU v7x, 32 devices: a whole 2x2x4 slice. The times are simulated.
32 devices in a mesh: pix: 16 (over z, y, core), chan: 2 (over x).
Axes of the slice: x: 2, y: 2, z: 4, core: 2. Of those that a mesh axis runs over, the one named last changes fastest.
Arguments:
- spectra: float32 [32768, 4096], P('pix', 'chan'), may hold values from 0.1 to 3
- coeffs: float32 [32, 32768], P(None, 'pix'), may hold values from 0.05 to 0.5
- endmembers: float32 [32, 4096], P(None, 'chan'), may hold values from 0.05 to 0.5
- pixel_mask: int32 [32768], P('pix'), may hold values from 0 to 1
- labels: int32 [32768], P('pix'), may hold values from 0 to 23
Outputs:
- new_coeffs: float32 [32, 32768], P(None, 'pix')
- new_endmembers: float32 [32, 4096], P(None, 'chan')
- centroids: float32 [24, 4096], P(None, 'chan')
- distances: float32 [32768], P('pix')
All inputs are finite; a program needn't handle non-finite values.
Results may differ from a plain program's by a relative error of at most 0.0003.
Values sent between devices are 32-bit elements; how exact they have to be, the bound alone decides.
No kernel may reach another device: no remote copies, remote signals or barrier semaphores. Data moves between devices by JAX's collectives and lax.ppermute only.
A program may use at most 64 MiB of HBM per device.

v0:
```python
import jax
import jax.numpy as jnp
from jax import lax
from jax.sharding import PartitionSpec as P

PHASES = 24
EPSILON = 1e-06


def product(left, right):
    return jnp.dot(left, right, precision=lax.Precision.HIGHEST, preferred_element_type=jnp.float32)


def contract(left, right, left_dim, right_dim):
    return lax.dot_general(
        left,
        right,
        (((left_dim,), (right_dim,)), ((), ())),
        precision=lax.Precision.HIGHEST,
        preferred_element_type=jnp.float32,
    )


def local(spectra, coeffs, endmembers, pixel_mask, labels):
    channels_total = endmembers.shape[1] * lax.axis_size("chan")
    local_numer = contract(endmembers, spectra, 1, 1)
    local_gram = contract(endmembers, endmembers, 1, 1)
    numer_coeff, gram_all = lax.psum((local_numer, local_gram), "chan")
    new_coeffs = coeffs * numer_coeff / (product(gram_all, coeffs) + EPSILON)
    weights = pixel_mask.astype(jnp.float32)
    weighted = new_coeffs * weights[None, :]
    onehot = (labels[None, :] == jnp.arange(PHASES, dtype=jnp.int32)[:, None]).astype(jnp.float32)
    picked = onehot * weights[None, :]
    numer_end, outer_gram, phase_sums, phase_counts = lax.psum(
        (
            product(weighted, spectra),
            contract(weighted, new_coeffs, 1, 1),
            contract(picked, new_coeffs, 1, 1),
            jnp.sum(picked, axis=1),
        ),
        "pix",
    )
    new_endmembers = endmembers * numer_end / (product(outer_gram, endmembers) + EPSILON)
    phase_means = phase_sums / (phase_counts + 1.0)[:, None]
    centroids = product(phase_means, new_endmembers)
    gram_updated = lax.psum(contract(new_endmembers, new_endmembers, 1, 1), "chan")
    offset = new_coeffs - contract(phase_means, onehot, 0, 0)
    distance = jnp.sum(offset * product(gram_updated, offset), axis=0) / channels_total
    return (new_coeffs, new_endmembers, centroids, distance)


def solution(mesh):
    placed = (P("pix", "chan"), P(None, "pix"), P(None, "chan"), P("pix"), P("pix"))
    return jax.shard_map(
        local,
        mesh=mesh,
        in_specs=placed,
        out_specs=(P(None, "pix"), P(None, "chan"), P(None, "chan"), P("pix")),
        check_vma=False,
    )
```

profile of v0, /device:TPU:0, one launch (start us, length us, event | category | flops | bytes accessed | tf_op | source)
XLA Modules:
  0.0 179.4 jit_solution(9026116440240854238)
XLA Ops:
  7.2 0.0 copy-start.1
  7.2 0.0 copy-start.4
  7.2 0.0 copy-start.3
  7.2 0.0 copy-start.5
  7.2 0.0 all-reduce.4.cloned.1.call-start
  7.3 21.4 %fusion.17 = f32[32,2048]{1,0:T(8,128)} fusion(f32[32,2048]{1,0:T(8,128)} %param.7, f32[2048,2048]{1,0:T(8,128)} %param.5), kind=kOutput, calls=%fused_computation.26 | convolution fusion | flops 1610612736 | bytes 17301504 | tf_op jit(solution)/shard_map/dot_general | solution.py:15
  28.6 0.0 all-reduce.4.cloned.1.call-update
  28.7 0.0 all-reduce.6.cloned.1.call-start
  28.7 0.0 copy-done.4
  28.7 0.0 copy-done.1
  28.7 0.4 fusion.18
  29.1 9.7 %psum.50 = f32[32,32]{1,0:T(8,128)S(1)} all-reduce(f32[32,32]{1,0:T(8,128)S(1)} %fusion.18), channel_id=1, replica_groups=mesh['pix'=16,'chan'=2] {'chan'}, use_global_device_ids=true, to_apply=%region_1.0 | all-reduce | flops 1024 | bytes 8192 | tf_op jit(solution)/shard_map/psum | solution.py:28
  38.8 0.0 copy-done.3
  38.8 0.1 select_reduce_fusion
  38.9 16.0 %all-reduce.4.cloned.1.call-done = f32[32,2048]{1,0:T(8,128)} async-done(((f32[32,2048]{1,0:T(8,128)}), f32[32,2048]{1,0:T(8,128)}) %all-reduce.4.cloned.1.call-update) | async-done | bytes 262160 | tf_op jit(solution)/shard_map/psum | solution.py:28
  54.9 1.3 fusion.1
  56.3 0.0 copy-start
  56.3 0.3 fusion.3
  56.6 0.3 fusion.7
  56.9 13.9 %fusion.5 = f32[32,2048]{1,0:T(8,128)} fusion(f32[2048,2048]{1,0:T(8,128)} %param.5, f32[32,2048]{1,0:T(8,128)S(1)} %fusion.1, f32[2048]{0:T(1024)S(1)} %convert_element_type.4), kind=kOutput, calls=%fused_computation.9 | convolution fusion | flops 1610678272 | bytes 17309696 | tf_op jit(solution)/shard_map/dot_general | solution.py:11
  70.8 0.0 all-reduce.6.cloned.1.call-update
  70.8 60.7 %all-reduce = (f32[32,32]{1,0:T(8,128)S(1)}, f32[24,32]{1,0:T(8,128)S(1)}, f32[24]{0:T(128)S(1)}) all-reduce(f32[32,32]{1,0:T(8,128)S(1)} %fusion.3, f32[24,32]{1,0:T(8,128)S(1)} %fusion.7, f32[24]{0:T(128)S(1)} %select_reduce_fusion), channel_id=1, replica_groups=mesh['pix'=16,'chan'=2] {'pix'}, use_global_device_ids=true, to_apply=%region_3.0 | all-reduce | flops 1816 | bytes 14528 | tf_op jit(solution)/shard_map/psum | solution.py:34
  131.5 0.4 convolution_subtract_fusion
  131.9 28.7 %all-reduce.6.cloned.1.call-done = f32[32,2048]{1,0:T(8,128)} async-done(((f32[32,2048]{1,0:T(8,128)}), f32[32,2048]{1,0:T(8,128)}) %all-reduce.6.cloned.1.call-update) | async-done | bytes 262160 | tf_op jit(solution)/shard_map/psum | solution.py:34
  160.7 1.3 fusion
  162.0 0.0 copy-start.2
  162.0 1.1 fusion.15
  163.1 0.4 fusion.19
  163.4 8.1 %psum.55 = f32[32,32]{1,0:T(8,128)S(1)} all-reduce(f32[32,32]{1,0:T(8,128)S(1)} %fusion.19), channel_id=1, replica_groups=mesh['pix'=16,'chan'=2] {'chan'}, use_global_device_ids=true, to_apply=%region_7.0 | all-reduce | flops 1024 | bytes 8192 | tf_op jit(solution)/shard_map/psum | solution.py:46
  171.5 0.4 fusion.2
  171.9 0.6 broadcast_multiply_fusion
  172.5 0.0 copy-done
  (4 shorter events, 0.0 us)
Async XLA Ops:
  7.2 21.6 %copy-start.1 = (f32[32,2048]{1,0:T(8,128)S(1)}, f32[32,2048]{1,0:T(8,128)}, u32[]{:S(2)}) copy-start(f32[32,2048]{1,0:T(8,128)} %param.7) | copy-start | bytes 786436
  7.2 21.5 %copy-start.4 = (s32[2048]{0:T(1024)S(1)}, s32[2048]{0:T(1024)}, u32[]{:S(2)}) copy-start(s32[2048]{0:T(1024)} %param.8) | copy-start | bytes 24580
  7.2 31.6 %copy-start.3 = (s32[2048]{0:T(1024)S(1)}, s32[2048]{0:T(1024)}, u32[]{:S(2)}) copy-start(s32[2048]{0:T(1024)} %param.9) | copy-start | bytes 24580
  7.2 47.7 %copy-start.5 = (f32[32,2048]{1,0:T(8,128)S(1)}, f32[32,2048]{1,0:T(8,128)}, u32[]{:S(2)}) copy-start(f32[32,2048]{1,0:T(8,128)} %param.6) | copy-start | bytes 786436
  7.2 47.7 %all-reduce.4.cloned.1.call-start = ((), (), s32[]{:S(2)}) async-start(), calls=%async_computation | async-start | bytes 524288 | tf_op jit(solution)/shard_map/psum | solution.py:28
  28.7 132.0 %all-reduce.6.cloned.1.call-start = ((), (), s32[]{:S(2)}) async-start(), calls=%async_computation.1 | async-start | bytes 524288 | tf_op jit(solution)/shard_map/psum | solution.py:34
  56.3 116.3 %copy-start = (f32[32,2048]{1,0:T(8,128)}, f32[32,2048]{1,0:T(8,128)S(1)}, u32[]{:S(2)}) copy-start(f32[32,2048]{1,0:T(8,128)S(1)} %fusion.1) | copy-start | bytes 786436
  162.0 10.5 %copy-start.2 = (f32[32,2048]{1,0:T(8,128)}, f32[32,2048]{1,0:T(8,128)S(1)}, u32[]{:S(2)}) copy-start(f32[32,2048]{1,0:T(8,128)S(1)} %fusion) | copy-start | bytes 786436
Sparse Core Ops, SparseCore 0:
  28.8 26.0 all-reduce.3
  70.9 89.7 all-reduce.5
where the time goes:
time: 180 us; the launch traced here: 179 us
  blocking collectives  78.5 us (44%)
  waiting for transfers between devices  44.8 us (25%)
  matrix products  41 us (23%)
  between operations  14.2 us (8%)
    psum x1, blocking collectives, local(): lax.psum((product(weighted, spectra), contract(weighted, new_coeffs, 1, 1...  60.7 us
    psum x1, waiting for transfers between devices, local(): lax.psum((product(weighted, spectra), contract(weighted, new_coeffs, 1, 1...  28.7 us
    dot_general x6, matrix products, contract(): lax.dot_general(left, right, (((left_dim,), (right_dim,)), ((), ())), pre...  23.1 us
    dot_general x5, matrix products, product(): jnp.dot(left, right, precision=lax.Precision.HIGHEST, preferred_element_t...  17.9 us
    psum x1, waiting for transfers between devices, local(): numer_coeff, gram_all = lax.psum((local_numer, local_gram), 'chan')  16 us
    psum x1, blocking collectives, local(): numer_coeff, gram_all = lax.psum((local_numer, local_gram), 'chan')  9.69 us
    psum x1, blocking collectives, local(): lax.psum(contract(new_endmembers, new_endmembers, 1, 1), 'chan')  8.11 us
  transfers between devices with their start and end apart: 2, of which 2 were waited for; matrix products, arithmetic and copies ran while one was open for 1% of the time, Pallas kernels for 0%

commit v1 on v0

--- a/solution.py
+++ b/solution.py
@@ -43,7 +43,9 @@
     new_endmembers = endmembers * numer_end / (product(outer_gram, endmembers) + EPSILON)
     phase_means = phase_sums / (phase_counts + 1.0)[:, None]
     centroids = product(phase_means, new_endmembers)
-    gram_updated = lax.psum(contract(new_endmembers, new_endmembers, 1, 1), "chan")
+    gram_updated = jnp.sum(
+        lax.all_gather(contract(new_endmembers, new_endmembers, 1, 1), "chan"), 0
+    )
     offset = new_coeffs - contract(phase_means, onehot, 0, 0)
     distance = jnp.sum(offset * product(gram_updated, offset), axis=0) / channels_total
     return (new_coeffs, new_endmembers, centroids, distance)

time: 180 us -> 233 us (1.29)
  waiting for transfers between devices: 44.8 us -> 102 us
  blocking collectives: 78.5 us -> 74.7 us
    psum x1, waiting for transfers between devices: 28.7 us -> 85.8 us  [local(): lax.psum((product(weighted, spectra), contract(weighted, new_coeffs, 1, 1...]
    psum x1 -> x0, blocking collectives: 8.11 us -> none  [local(): lax.psum(contract(new_endmembers, new_endmembers, 1, 1), 'chan')]
    all_gather x0 -> x1, blocking collectives: none -> 4.39 us  [local(): lax.all_gather(contract(new_endmembers, new_endmembers, 1, 1), 'chan')]
  transfers between devices with their start and end apart: 2 -> 2, of which waited for: 2 -> 2; matrix products, arithmetic and copies ran while one was open for 1% -> 0% of each run, Pallas kernels for 0% -> 0%
where the time goes in v1:
time: 233 us
  waiting for transfers between devices  102 us (44%)
  blocking collectives  74.7 us (32%)
  matrix products  41 us (18%)
  between operations  14.2 us (6%)
    psum x1, waiting for transfers between devices, local(): lax.psum((product(weighted, spectra), contract(weighted, new_coeffs, 1, 1...  85.8 us
    psum x1, blocking collectives, local(): lax.psum((product(weighted, spectra), contract(weighted, new_coeffs, 1, 1...  60.7 us
    dot_general x6, matrix products, contract(): lax.dot_general(left, right, (((left_dim,), (right_dim,)), ((), ())), pre...  23.1 us
    dot_general x5, matrix products, product(): jnp.dot(left, right, precision=lax.Precision.HIGHEST, preferred_element_t...  17.9 us
    psum x1, waiting for transfers between devices, local(): numer_coeff, gram_all = lax.psum((local_numer, local_gram), 'chan')  16 us
    psum x1, blocking collectives, local(): numer_coeff, gram_all = lax.psum((local_numer, local_gram), 'chan')  9.69 us
  transfers between devices with their start and end apart: 2, of which 2 were waited for; matrix products, arithmetic and copies ran while one was open for 0% of the time, Pallas kernels for 0%

profile of v1, /device:TPU:0, one launch (start us, length us, event | category | flops | bytes accessed | tf_op | source)
XLA Modules:
  0.0 232.7 jit_solution(4842331529808148425)
XLA Ops:
  7.2 0.0 copy-start.1
  7.2 0.0 copy-start.4
  7.2 0.0 copy-start.3
  7.2 0.0 copy-start.5
  7.2 0.0 all-reduce.4.cloned.1.call-start
  7.3 21.4 %fusion.17 = f32[32,2048]{1,0:T(8,128)} fusion(f32[32,2048]{1,0:T(8,128)} %param.7, f32[2048,2048]{1,0:T(8,128)} %param.5), kind=kOutput, calls=%fused_computation.26 | convolution fusion | flops 1610612736 | bytes 17301504 | tf_op jit(solution)/shard_map/dot_general | solution.py:15
  28.6 0.0 all-reduce.4.cloned.1.call-update
  28.7 0.0 all-reduce.6.cloned.1.call-start
  28.7 0.0 copy-done.4
  28.7 0.0 copy-done.1
  28.7 0.4 fusion.18
  29.1 9.7 %psum.43 = f32[32,32]{1,0:T(8,128)S(1)} all-reduce(f32[32,32]{1,0:T(8,128)S(1)} %fusion.18), channel_id=1, replica_groups=mesh['pix'=16,'chan'=2] {'chan'}, use_global_device_ids=true, to_apply=%region_1.0 | all-reduce | flops 1024 | bytes 8192 | tf_op jit(solution)/shard_map/psum | solution.py:28
  38.8 0.0 copy-done.3
  38.8 0.1 select_reduce_fusion
  38.9 16.0 %all-reduce.4.cloned.1.call-done = f32[32,2048]{1,0:T(8,128)} async-done(((f32[32,2048]{1,0:T(8,128)}), f32[32,2048]{1,0:T(8,128)}) %all-reduce.4.cloned.1.call-update) | async-done | bytes 262160 | tf_op jit(solution)/shard_map/psum | solution.py:28
  54.9 1.3 fusion.1
  56.3 0.0 copy-start
  56.3 0.3 fusion.7
  56.6 0.4 fusion.3
  56.9 13.8 %fusion.5 = f32[32,2048]{1,0:T(8,128)} fusion(f32[2048,2048]{1,0:T(8,128)} %param.5, f32[32,2048]{1,0:T(8,128)S(1)} %fusion.1, f32[2048]{0:T(1024)S(1)} %convert_element_type.4), kind=kOutput, calls=%fused_computation.9 | convolution fusion | flops 1610678272 | bytes 17309696 | tf_op jit(solution)/shard_map/dot_general | solution.py:11
  70.8 60.7 %all-reduce = (f32[32,32]{1,0:T(8,128)S(1)}, f32[24,32]{1,0:T(8,128)S(1)}, f32[24]{0:T(128)S(1)}) all-reduce(f32[32,32]{1,0:T(8,128)S(1)} %fusion.3, f32[24,32]{1,0:T(8,128)S(1)} %fusion.7, f32[24]{0:T(128)S(1)} %select_reduce_fusion), channel_id=1, replica_groups=mesh['pix'=16,'chan'=2] {'pix'}, use_global_device_ids=true, to_apply=%region_3.0 | all-reduce | flops 1816 | bytes 14528 | tf_op jit(solution)/shard_map/psum | solution.py:34
  131.5 0.0 all-reduce.6.cloned.1.call-update
  131.5 0.4 convolution_subtract_fusion
  131.9 85.8 %all-reduce.6.cloned.1.call-done = f32[32,2048]{1,0:T(8,128)} async-done(((f32[32,2048]{1,0:T(8,128)}), f32[32,2048]{1,0:T(8,128)}) %all-reduce.6.cloned.1.call-update) | async-done | bytes 262160 | tf_op jit(solution)/shard_map/psum | solution.py:34
  217.7 1.3 fusion
  219.0 0.0 copy-start.2
  219.0 0.3 fusion.19
  219.4 1.1 fusion.15
  220.4 4.4 %all-gather = f32[64,32]{1,0:T(8,128)S(1)} all-gather(f32[32,32]{1,0:T(8,128)S(1)} %fusion.19), channel_id=2, replica_groups=mesh['pix'=16,'chan'=2] {'chan'}, dimensions={0}, use_global_device_ids=true | all-gather | bytes 12288 | tf_op jit(solution)/shard_map/all_gather | solution.py:47
  224.8 0.4 fusion.2
  225.2 0.6 broadcast_multiply_fusion
  225.8 0.0 copy-done.2
  (5 shorter events, 0.0 us)
Async XLA Ops:
  7.2 21.6 %copy-start.1 = (f32[32,2048]{1,0:T(8,128)S(1)}, f32[32,2048]{1,0:T(8,128)}, u32[]{:S(2)}) copy-start(f32[32,2048]{1,0:T(8,128)} %param.7) | copy-start | bytes 786436
  7.2 21.5 %copy-start.4 = (s32[2048]{0:T(1024)S(1)}, s32[2048]{0:T(1024)}, u32[]{:S(2)}) copy-start(s32[2048]{0:T(1024)} %param.8) | copy-start | bytes 24580
  7.2 31.6 %copy-start.3 = (s32[2048]{0:T(1024)S(1)}, s32[2048]{0:T(1024)}, u32[]{:S(2)}) copy-start(s32[2048]{0:T(1024)} %param.9) | copy-start | bytes 24580
  7.2 47.7 %copy-start.5 = (f32[32,2048]{1,0:T(8,128)S(1)}, f32[32,2048]{1,0:T(8,128)}, u32[]{:S(2)}) copy-start(f32[32,2048]{1,0:T(8,128)} %param.6) | copy-start | bytes 786436
  7.2 47.7 %all-reduce.4.cloned.1.call-start = ((), (), s32[]{:S(2)}) async-start(), calls=%async_computation | async-start | bytes 524288 | tf_op jit(solution)/shard_map/psum | solution.py:28
  28.7 189.0 %all-reduce.6.cloned.1.call-start = ((), (), s32[]{:S(2)}) async-start(), calls=%async_computation.1 | async-start | bytes 524288 | tf_op jit(solution)/shard_map/psum | solution.py:34
  56.3 169.6 %copy-start = (f32[32,2048]{1,0:T(8,128)}, f32[32,2048]{1,0:T(8,128)S(1)}, u32[]{:S(2)}) copy-start(f32[32,2048]{1,0:T(8,128)S(1)} %fusion.1) | copy-start | bytes 786436
  219.0 6.8 %copy-start.2 = (f32[32,2048]{1,0:T(8,128)}, f32[32,2048]{1,0:T(8,128)S(1)}, u32[]{:S(2)}) copy-start(f32[32,2048]{1,0:T(8,128)S(1)} %fusion) | copy-start | bytes 786436
Sparse Core Ops, SparseCore 0:
  28.8 26.0 all-reduce.3
  131.6 86.0 all-reduce.5
